TPU v7x, 32 devices: a whole 2x2x4 slice. The times are simulated.
32 devices in a mesh: ctx: 2 (over core), shard: 16 (over z, y, x).
Axes of the slice: x: 2, y: 2, z: 4, core: 2. Of those that a mesh axis runs over, the one named last changes fastest.
Arguments:
- tokens: bfloat16 [2, 16, 1024, 768], P(None, 'shard', 'ctx'), may hold values from -6 to 6
- cotangent: bfloat16 [2, 16, 1024, 768], P(None, 'shard', 'ctx'), may hold values from -6 to 6
- segment_ids: int32 [2, 16, 1024], P(None, 'shard', 'ctx'), may hold values from 0 to 1, never falling along the last dimension, each value on 1 to 896 neighbouring positions
- padding: int32 [2, 16, 1024], P(None, 'shard', 'ctx'), may hold values 0 or 1
- routes: int32 [2, 16, 1024, 1], P(None, 'shard', 'ctx'), may hold values from 0 to 15; in each aligned block of 512 rows (0 to 511, 512 to 1023, ..., all dimensions but the last counted through in order) at most 64 rows name the same one
- norm_one_gain: bfloat16 [768], replicated, may hold values from 0.5 to 1.5
- qkv_weight: bfloat16 [768, 2304], P('shard'), may hold values from -0.21875 to 0.21875
- out_weight: bfloat16 [768, 768], P('shard'), may hold values from -1.75 to 1.75
- norm_two_gain: bfloat16 [768], replicated, may hold values from 0.5 to 1.5
- centroids: bfloat16 [768, 16], replicated, may hold values from -0.15625 to 0.15625
- expert_in: bfloat16 [16, 768, 3072], P('shard'), may hold values from -0.21875 to 0.21875
- expert_out: bfloat16 [16, 3072, 768], P('shard'), may hold values from -0.21875 to 0.21875
Outputs:
- block_out: bfloat16 [2, 16, 1024, 768], P(None, 'shard', 'ctx')
- grad_tokens: float32 [2, 16, 1024, 768], P(None, 'shard', 'ctx')
- grad_norm_one: float32 [768], P(('ctx', 'shard'))
- grad_qkv: float32 [768, 2304], P(('ctx', 'shard'))
- grad_out_proj: float32 [768, 768], P(('ctx', 'shard'))
- grad_norm_two: float32 [768], P(('ctx', 'shard'))
- grad_centroids: float32 [768, 16], P(('ctx', 'shard'))
- grad_expert_in: float32 [16, 768, 3072], P('shard', None, 'ctx')
- grad_expert_out: float32 [16, 3072, 768], P('shard', 'ctx')
Inputs may be any that keep to these rules, and one draw needn't show every extreme that they name: `segment_ids`: segment ids never fall along a sequence; each sequence holds two documents, each of at least 128 and at most 896 positions; where the split falls varies from sequence to sequence. `routes`: within each aligned block of 512 positions of a sequence, no expert is named more than 64 times; some block names some expert exactly 64 times.
All inputs are finite; a program needn't handle non-finite values. No bound on the sum of `padding` on one device may be relied on, other than what follows from the above.
Results may differ from a plain program's by a relative error of at most 0.013.
Values may be sent and summed in bfloat16 or wider, within the bound.
A program may use at most 384 MiB of HBM per device.

v0:
```python
import jax
import jax.numpy as jnp
from jax import lax
from jax.sharding import PartitionSpec as P

D = 768
HEADS = 12
HEAD_DIM = 64
FF = 3072
MICRO = 2
EPSILON = 1e-05
NEGATIVE = -1e30
HIGH = lax.Precision.HIGHEST


def layer_norm(values, gain_vec):
    centre = values - jnp.mean(values, axis=1, keepdims=True)
    spread = jnp.mean(centre * centre, axis=1, keepdims=True)
    return centre * lax.rsqrt(spread + EPSILON) * gain_vec


def gelu_tanh(values):
    return jax.nn.gelu(values, approximate=True)


def masked_scores(queries, key_heads, query_pos, key_pos, query_doc, key_doc, key_pad):
    scores = jnp.einsum(
        "qhd,khd->hqk", queries, key_heads, preferred_element_type=jnp.float32
    ) * HEAD_DIM ** (-0.5)
    allowed = (query_doc[:, None] == key_doc[None, :]) & (key_pos[None, :] <= query_pos[:, None])
    allowed = allowed & ((key_pad[None, :] == 1) | (key_pos[None, :] == query_pos[:, None]))
    return jnp.where(allowed[None], scores, NEGATIVE)


def rows_first(left, right):
    return lax.dot_general(
        left, right, (((0,), (0,)), ((), ())), preferred_element_type=jnp.float32
    )


def rows_last(left, right):
    return lax.dot_general(
        left, right, (((1,), (1,)), ((), ())), preferred_element_type=jnp.float32
    )


def body(
    tokens,
    cotangent,
    segment_ids,
    padding,
    routes,
    norm_one_gain,
    qkv_weight,
    out_weight,
    norm_two_gain,
    centroids,
    expert_in,
    expert_out,
):
    local_len = tokens.shape[2]
    experts = centroids.shape[1]
    capacity = max(2, 2 * local_len // experts)
    seq_len = local_len * lax.axis_size("ctx")
    qkv_full, out_full = (
        lax.all_gather(qkv_weight, "shard", axis=0, tiled=True),
        lax.all_gather(out_weight, "shard", axis=0, tiled=True),
    )
    gain_one = norm_one_gain.astype(jnp.float32)
    gain_two = norm_two_gain.astype(jnp.float32)
    centre_f = centroids.astype(jnp.float32)
    up_local = expert_in[0]
    down_local = expert_out[0]
    query_pos = lax.axis_index("ctx") * local_len + jnp.arange(local_len, dtype=jnp.int32)
    all_pos = jnp.arange(seq_len, dtype=jnp.int32)
    slot_ids = jnp.arange(experts * capacity, dtype=jnp.int32)
    expert_ids = jnp.arange(experts, dtype=jnp.int32)
    score_scale = HEAD_DIM ** (-0.5)
    grad_qkv_sum = jnp.zeros((D, 3 * D), jnp.float32)
    grad_out_sum = jnp.zeros((D, D), jnp.float32)
    grad_one_sum = jnp.zeros((D,), jnp.float32)
    grad_two_sum = jnp.zeros((D,), jnp.float32)
    grad_centre = jnp.zeros((D, experts), jnp.float32)
    grad_up_sum = jnp.zeros((D, FF), jnp.float32)
    grad_down_sum = jnp.zeros((D, FF), jnp.float32)
    block_list = []
    input_list = []
    for micro_index in range(MICRO):
        inputs = tokens[micro_index, 0].astype(jnp.float32)
        doc_ids = segment_ids[micro_index, 0]
        pad_mask = padding[micro_index, 0]
        route_ids = routes[micro_index, 0, :, 0]
        normed_one, norm_one_back = jax.vjp(layer_norm, inputs, gain_one)
        first_bf = normed_one.astype(jnp.bfloat16)
        qkv = jnp.dot(first_bf, qkv_full, preferred_element_type=jnp.float32)
        queries = qkv[:, :D].astype(jnp.bfloat16)
        key_rows = qkv[:, D : 2 * D].astype(jnp.bfloat16)
        value_rows = qkv[:, 2 * D :].astype(jnp.bfloat16)
        key_all, value_all, doc_all, pad_all = (
            lax.all_gather(key_rows, "ctx", axis=0, tiled=True),
            lax.all_gather(value_rows, "ctx", axis=0, tiled=True),
            lax.all_gather(doc_ids, "ctx", axis=0, tiled=True),
            lax.all_gather(pad_mask, "ctx", axis=0, tiled=True),
        )
        query_heads = queries.reshape(local_len, HEADS, HEAD_DIM)
        key_heads = key_all.reshape(seq_len, HEADS, HEAD_DIM)
        value_heads = value_all.reshape(seq_len, HEADS, HEAD_DIM)
        scores = masked_scores(
            query_heads, key_heads, query_pos, all_pos, doc_ids, doc_all, pad_all
        )
        row_max = jnp.max(scores, axis=2, keepdims=True)
        weights = jnp.exp(scores - row_max)
        row_total = jnp.sum(weights, axis=2, keepdims=True)
        probs_now = weights / row_total
        log_total = row_max + jnp.log(row_total)
        attended = jnp.einsum(
            "hqk,khd->qhd",
            probs_now.astype(jnp.bfloat16),
            value_heads,
            preferred_element_type=jnp.float32,
        )
        attended = attended.reshape(local_len, D).astype(jnp.bfloat16)
        residual = inputs + jnp.dot(attended, out_full, preferred_element_type=jnp.float32)
        normed_two, norm_two_back = jax.vjp(layer_norm, residual, gain_two)
        second_bf = normed_two.astype(jnp.bfloat16)
        choose_mask = route_ids[:, None] == expert_ids[None, :]
        choose_f = choose_mask.astype(jnp.float32)
        logit = jnp.sum(
            jnp.dot(second_bf, centroids, preferred_element_type=jnp.float32) * choose_f, axis=1
        )
        gate_value = jax.nn.sigmoid(logit)
        choose_int = choose_mask.astype(jnp.int32)
        counts = jnp.cumsum(choose_int, axis=0)
        slot_rank = jnp.sum(counts * choose_int, axis=1) - 1
        target = route_ids * capacity + slot_rank
        dispatch = (slot_ids[:, None] == target[None, :]).astype(jnp.bfloat16)
        outbound = jnp.dot(dispatch, second_bf, preferred_element_type=jnp.float32).astype(
            jnp.bfloat16
        )
        outbound = outbound.reshape(experts, capacity, D)
        received = lax.all_to_all(outbound, "shard", split_axis=0, concat_axis=0, tiled=True)
        slot_rows = received.reshape(-1, D)
        upward = jnp.dot(slot_rows, up_local, preferred_element_type=jnp.float32)
        hidden = gelu_tanh(upward).astype(jnp.bfloat16)
        result = jnp.dot(hidden, down_local, preferred_element_type=jnp.float32).astype(
            jnp.bfloat16
        )
        returned = lax.all_to_all(
            result.reshape(received.shape), "shard", split_axis=0, concat_axis=0, tiled=True
        )
        returned, received, upward = (
            returned,
            received,
            upward.reshape(received.shape[0], received.shape[1], FF),
        )
        expert_rows = rows_first(dispatch, returned.reshape(experts * capacity, D))
        block_list.append((residual + gate_value[:, None] * expert_rows).astype(jnp.bfloat16))
        grad_out = cotangent[micro_index, 0].astype(jnp.float32)
        grad_gate = jnp.sum(grad_out * expert_rows, axis=1)
        grad_logit = grad_gate * gate_value * (1.0 - gate_value)
        grad_rows = (gate_value[:, None] * grad_out).astype(jnp.bfloat16)
        grad_outbound = jnp.dot(dispatch, grad_rows, preferred_element_type=jnp.float32).astype(
            jnp.bfloat16
        )
        grad_received = lax.all_to_all(
            grad_outbound.reshape(experts, capacity, D),
            "shard",
            split_axis=0,
            concat_axis=0,
            tiled=True,
        )
        grad_result = grad_received.reshape(-1, D)
        hidden_again, gelu_back = jax.vjp(gelu_tanh, upward.reshape(-1, FF))
        grad_down_sum = grad_down_sum + rows_first(grad_result, hidden_again.astype(jnp.bfloat16))
        grad_hidden = rows_last(grad_result, down_local)
        grad_upward = gelu_back(grad_hidden)[0].astype(jnp.bfloat16)
        grad_up_sum = grad_up_sum + rows_first(received.reshape(-1, D), grad_upward)
        grad_send = (
            rows_last(grad_upward, up_local).astype(jnp.bfloat16).reshape(grad_received.shape)
        )
        grad_back = lax.all_to_all(grad_send, "shard", split_axis=0, concat_axis=0, tiled=True)
        grad_second = rows_first(dispatch, grad_back.reshape(experts * capacity, D))
        grad_second = grad_second + grad_logit[:, None] * jnp.dot(
            choose_f, centre_f.T, precision=HIGH
        )
        grad_centre = grad_centre + jnp.dot(
            second_bf.astype(jnp.float32).T, choose_f * grad_logit[:, None], precision=HIGH
        )
        grad_resid_norm, grad_two_term = norm_two_back(grad_second)
        grad_residual = grad_out + grad_resid_norm
        grad_two_sum = grad_two_sum + grad_two_term
        grad_branch = grad_residual.astype(jnp.bfloat16)
        grad_out_sum = grad_out_sum + rows_first(attended, grad_branch)
        grad_attend = (
            rows_last(grad_branch, out_full)
            .astype(jnp.bfloat16)
            .reshape(local_len, HEADS, HEAD_DIM)
        )
        probs_again = jnp.exp(
            masked_scores(query_heads, key_heads, query_pos, all_pos, doc_ids, doc_all, pad_all)
            - log_total
        )
        grad_probs = jnp.einsum(
            "qhd,khd->hqk", grad_attend, value_heads, preferred_element_type=jnp.float32
        )
        row_terms = jnp.sum(probs_again * grad_probs, axis=2, keepdims=True)
        grad_scores = (probs_again * (grad_probs - row_terms)).astype(jnp.bfloat16)
        grad_query = (
            jnp.einsum("hqk,khd->qhd", grad_scores, key_heads, preferred_element_type=jnp.float32)
            * score_scale
        )
        grad_key_all = (
            jnp.einsum("hqk,qhd->khd", grad_scores, query_heads, preferred_element_type=jnp.float32)
            * score_scale
        )
        grad_value_all = jnp.einsum(
            "hqk,qhd->khd",
            probs_again.astype(jnp.bfloat16),
            grad_attend,
            preferred_element_type=jnp.float32,
        )
        grad_key, grad_value = (
            lax.psum_scatter(
                grad_key_all.reshape(seq_len, D).astype(jnp.bfloat16),
                "ctx",
                scatter_dimension=0,
                tiled=True,
            ).astype(jnp.float32),
            lax.psum_scatter(
                grad_value_all.reshape(seq_len, D).astype(jnp.bfloat16),
                "ctx",
                scatter_dimension=0,
                tiled=True,
            ).astype(jnp.float32),
        )
        grad_qkv_rows = jnp.concatenate(
            [grad_query.reshape(local_len, D), grad_key, grad_value], axis=1
        ).astype(jnp.bfloat16)
        grad_qkv_sum = grad_qkv_sum + rows_first(first_bf, grad_qkv_rows)
        grad_first = rows_last(grad_qkv_rows, qkv_full)
        grad_in_norm, grad_one_term = norm_one_back(grad_first)
        grad_one_sum = grad_one_sum + grad_one_term
        input_list.append(grad_residual + grad_in_norm)
    dense_sums = (
        lax.psum_scatter(grad_one_sum, ("ctx", "shard"), scatter_dimension=0, tiled=True),
        lax.psum_scatter(grad_qkv_sum, ("ctx", "shard"), scatter_dimension=0, tiled=True),
        lax.psum_scatter(grad_out_sum, ("ctx", "shard"), scatter_dimension=0, tiled=True),
        lax.psum_scatter(grad_two_sum, ("ctx", "shard"), scatter_dimension=0, tiled=True),
        lax.psum_scatter(grad_centre, ("ctx", "shard"), scatter_dimension=0, tiled=True),
    )
    expert_sums = (
        lax.psum_scatter(
            grad_up_sum.astype(jnp.bfloat16), "ctx", scatter_dimension=1, tiled=True
        ).astype(jnp.float32),
        lax.psum_scatter(
            grad_down_sum.astype(jnp.bfloat16), "ctx", scatter_dimension=1, tiled=True
        ).astype(jnp.float32),
    )
    block_out = jnp.stack(block_list)[:, None]
    grad_tokens = jnp.stack(input_list)[:, None]
    return (
        block_out,
        grad_tokens,
        dense_sums[0],
        dense_sums[1],
        dense_sums[2],
        dense_sums[3],
        dense_sums[4],
        expert_sums[0][None],
        expert_sums[1].T[None],
    )


def solution(mesh):
    in_specs = (
        P(None, "shard", "ctx", None),
        P(None, "shard", "ctx", None),
        P(None, "shard", "ctx"),
        P(None, "shard", "ctx"),
        P(None, "shard", "ctx", None),
        P(),
        P("shard", None),
        P("shard", None),
        P(),
        P(),
        P("shard", None, None),
        P("shard", None, None),
    )
    out_specs = (
        P(None, "shard", "ctx", None),
        P(None, "shard", "ctx", None),
        P(("ctx", "shard")),
        P(("ctx", "shard"), None),
        P(("ctx", "shard"), None),
        P(("ctx", "shard")),
        P(("ctx", "shard"), None),
        P("shard", None, "ctx"),
        P("shard", "ctx", None),
    )
    return jax.shard_map(body, mesh=mesh, in_specs=in_specs, out_specs=out_specs, check_vma=False)
```

profile of v0, /device:TPU:0, one launch (start us, length us, event | category | flops | bytes accessed | tf_op | source)
XLA Modules:
  0.0 985.1 jit_solution(11996730696689875057)
XLA Ops:
  11.0 73.8 %all-gather.11.cloned.1.call-done = bf16[768,2304]{1,0:T(8,128)(2,1)} async-done(((bf16[48,2304]{1,0:T(8,128)(2,1)}), bf16[768,2304]{1,0:T(8,128)(2,1)}) %all-gather.11.cloned.1.call-update) | async-done | bytes 3538960 | tf_op jit(solution)/shard_map/all_gather | solution.py:66
  113.1 12.7 %fusion.27 = (f32[12,512]{1,0:T(8,128)S(1)}, f32[12,512,1024]{2,1,0:T(8,128)}) fusion(pred[512,1024]{1,0:T(8,128)(4,1)} %get-tuple-element.91, bf16[512,12,64]{0,2,1:T(8,128)(2,1)} %bitcast.293, bf16[1024,12,64]{0,2,1:T(8,128)(2,1)S(1)} %bitcast.289), kind=kOutput, calls=%fused_computation.45 | convolution fusion | flops 824174592 | bytes 28073984 | tf_op jit(solution)/shard_map/qhd,khd->hqk/dot_general | solution.py:27
  125.8 11.8 %fusion.1 = f32[12,512]{1,0:T(8,128)S(1)} fusion(f32[12,512]{1,0:T(8,128)S(1)} %get-tuple-element.96, f32[12,512,1024]{2,1,0:T(8,128)} %get-tuple-element.97, pred[512,1024]{1,0:T(8,128)(4,1)S(1)} %copy-done.14), kind=kLoop, calls=%fused_computation.13 | loop fusion | flops 25159680 | bytes 25739264 | tf_op jit(solution)/shard_map/reduce_sum | solution.py:113
  140.3 12.6 %fusion.112 = bf16[12,64,512]{2,1,0:T(8,128)(2,1)} fusion(bf16[1024,12,64]{0,2,1:T(8,128)(2,1)} %bitcast.299, f32[12,512]{1,0:T(8,128)S(1)} %fusion.1, f32[12,512]{1,0:T(8,128)S(1)} %get-tuple-element.96, f32[12,512,1024]{2,1,0:T(8,128)} %get-tuple-element.97, pred[512,1024]{1,0:T(8,128)(4,1)S(1)} %copy-done.15), kind=kOutput, calls=%fused_computation.162 | convolution fusion | flops 837156864 | bytes 28098560 | tf_op jit(solution)/shard_map/hqk,khd->qhd/dot_general | solution.py:116
  153.0 18.9 %all-gather.17.cloned.1.call-done = bf16[768,768]{1,0:T(8,128)(2,1)} async-done(((bf16[48,768]{1,0:T(8,128)(2,1)}), bf16[768,768]{1,0:T(8,128)(2,1)}) %all-gather.17.cloned.1.call-update) | async-done | bytes 1179664 | tf_op jit(solution)/shard_map/all_gather | solution.py:67
  185.3 15.0 %fusion.26 = (f32[12,512]{1,0:T(8,128)S(1)}, f32[12,512,1024]{2,1,0:T(8,128)}) fusion(pred[512,1024]{1,0:T(8,128)(4,1)} %get-tuple-element.90, bf16[512,12,64]{0,2,1:T(8,128)(2,1)} %bitcast.295, bf16[1024,12,64]{0,2,1:T(8,128)(2,1)} %bitcast.291), kind=kOutput, calls=%fused_computation.44 | convolution fusion | flops 824174592 | bytes 28073984 | tf_op jit(solution)/shard_map/qhd,khd->hqk/dot_general | solution.py:27
  200.4 11.8 %fusion = f32[12,512]{1,0:T(8,128)S(1)} fusion(f32[12,512]{1,0:T(8,128)S(1)} %get-tuple-element.92, f32[12,512,1024]{2,1,0:T(8,128)} %get-tuple-element.93, pred[512,1024]{1,0:T(8,128)(4,1)S(1)} %copy-done.17), kind=kLoop, calls=%fused_computation.12 | loop fusion | flops 25159680 | bytes 25739264 | tf_op jit(solution)/shard_map/reduce_sum | solution.py:113
  214.7 11.9 %fusion.113 = bf16[12,64,512]{2,1,0:T(8,128)(2,1)S(1)} fusion(bf16[1024,12,64]{0,2,1:T(8,128)(2,1)} %bitcast.301, f32[12,512]{1,0:T(8,128)S(1)} %fusion, f32[12,512]{1,0:T(8,128)S(1)} %get-tuple-element.92, f32[12,512,1024]{2,1,0:T(8,128)} %get-tuple-element.93, pred[512,1024]{1,0:T(8,128)(4,1)} %get-tuple-element.90), kind=kOutput, calls=%fused_computation.163 | convolution fusion | flops 837156864 | bytes 28098560 | tf_op jit(solution)/shard_map/hqk,khd->qhd/dot_general | solution.py:116
  241.5 30.6 %all-to-all-done.2 = bf16[16,64,768]{2,1,0:T(8,128)(2,1)} async-done(((bf16[16,64,768]{2,1,0:T(8,128)(2,1)}), bf16[16,64,768]{2,1,0:T(8,128)(2,1)}, u32[]{:S(2)}, u32[]{:S(2)}) %all-to-all-start.2) | async-done | bytes 1572896 | tf_op jit(solution)/shard_map/all_to_all | solution.py:141
  292.4 10.7 %fusion.91 = bf16[1024,768]{1,0:T(8,128)(2,1)} fusion(bf16[1,3072,768]{2,1,0:T(8,128)(2,1)} %param.23, f32[1024,3072]{1,0:T(8,128)S(1)} %fusion.40), kind=kOutput, calls=%fused_computation.128 | convolution fusion | flops 4860936192 | bytes 18874368 | tf_op jit(solution)/shard_map/dot_general | solution.py:145
  303.0 11.2 %all-to-all-done = bf16[16,64,768]{2,1,0:T(8,128)(2,1)} async-done(((bf16[16,64,768]{2,1,0:T(8,128)(2,1)}), bf16[16,64,768]{2,1,0:T(8,128)(2,1)}, u32[]{:S(2)}, u32[]{:S(2)}) %all-to-all-start) | async-done | bytes 1572896 | tf_op jit(solution)/shard_map/all_to_all | solution.py:141
  333.5 10.7 %fusion.88 = bf16[1024,768]{1,0:T(8,128)(2,1)} fusion(bf16[1,3072,768]{2,1,0:T(8,128)(2,1)} %param.23, f32[1024,3072]{1,0:T(8,128)S(1)} %fusion.42), kind=kOutput, calls=%fused_computation.127 | convolution fusion | flops 4860936192 | bytes 18874368 | tf_op jit(solution)/shard_map/dot_general | solution.py:145
  344.2 11.0 %all-to-all-done.3 = bf16[16,64,768]{2,1,0:T(8,128)(2,1)} async-done(((bf16[16,64,768]{2,1,0:T(8,128)(2,1)}), bf16[16,64,768]{2,1,0:T(8,128)(2,1)}, u32[]{:S(2)}, u32[]{:S(2)}) %all-to-all-start.3) | async-done | bytes 1572896 | tf_op jit(solution)/shard_map/all_to_all | solution.py:148
  367.0 29.4 %all-to-all-done.1 = bf16[16,64,768]{2,1,0:T(8,128)(2,1)} async-done(((bf16[16,64,768]{2,1,0:T(8,128)(2,1)}), bf16[16,64,768]{2,1,0:T(8,128)(2,1)}, u32[]{:S(2)}, u32[]{:S(2)}) %all-to-all-start.1) | async-done | bytes 1572896 | tf_op jit(solution)/shard_map/all_to_all | solution.py:148
  414.8 29.7 %all-to-all-done.6 = bf16[16,64,768]{2,1,0:T(8,128)(2,1)} async-done(((bf16[16,64,768]{2,1,0:T(8,128)(2,1)}), bf16[16,64,768]{2,1,0:T(8,128)(2,1)}, u32[]{:S(2)}, u32[]{:S(2)}) %all-to-all-start.6) | async-done | bytes 1572896 | tf_op jit(solution)/shard_map/all_to_all | solution.py:165
  452.2 15.4 %fusion.17 = bf16[1024,3072]{1,0:T(8,128)(2,1)S(1)} fusion(f32[1024,3072]{1,0:T(8,128)} %copy-done.93, bf16[1024,768]{1,0:T(8,128)(2,1)} %bitcast.53, bf16[1,3072,768]{2,1,0:T(8,128)(2,1)} %param.23), kind=kOutput, calls=%fused_computation.33 | convolution fusion | flops 4894752768 | bytes 25165824 | tf_op jit(solution)/shard_map/dot_general | solution.py:42
  493.2 14.2 %fusion.10 = bf16[1024,3072]{1,0:T(8,128)(2,1)S(1)} fusion(f32[1024,3072]{1,0:T(8,128)} %copy-done.94, bf16[1024,768]{1,0:T(8,128)(2,1)S(1)} %bitcast.309, bf16[1,3072,768]{2,1,0:T(8,128)(2,1)} %param.23), kind=kOutput, calls=%fused_computation.26 | convolution fusion | flops 4894752768 | bytes 25165824 | tf_op jit(solution)/shard_map/dot_general | solution.py:42
  540.2 27.5 %all-to-all-done.5 = bf16[16,64,768]{2,1,0:T(8,128)(2,1)} async-done(((bf16[16,64,768]{2,1,0:T(8,128)(2,1)}), bf16[16,64,768]{2,1,0:T(8,128)(2,1)}, u32[]{:S(2)}, u32[]{:S(2)}) %all-to-all-start.5) | async-done | bytes 1572896 | tf_op jit(solution)/shard_map/all_to_all | solution.py:181
  582.2 17.9 %multiply_reduce_fusion.1 = (f32[12,512]{1,0:T(8,128)S(1)}, f32[12,512,1024]{2,1,0:T(8,128)}) fusion(f32[12,512]{1,0:T(8,128)S(1)} %log_add_fusion.1, f32[12,512,1024]{2,1,0:T(8,128)} %get-tuple-element.93, pred[512,1024]{1,0:T(8,128)(4,1)S(1)} %copy-done.18, bf16[512,12,64]{0,2,1:T(8,128)(2,1)} %bitcast.307, bf16[1024,12,64]{0,2,1:T(8,128)(2,1)S(1)} %bitcast.302), kind=kOutput, calls=%fused_computation.4 | convolution fusion | flops 836757504 | bytes 53264384 | tf_op jit(solution)/shard_map/qhd,khd->hqk/dot_general | solution.py:203
  600.1 16.9 %multiply_convert_fusion.1 = bf16[12,512,1024]{2,1,0:T(8,128)(2,1)S(1)} fusion(f32[12,512,1024]{2,1,0:T(8,128)} %get-tuple-element.103, f32[12,512]{1,0:T(8,128)S(1)} %get-tuple-element.102, f32[12,512]{1,0:T(8,128)S(1)} %log_add_fusion.1, f32[12,512,1024]{2,1,0:T(8,128)} %get-tuple-element.93, pred[512,1024]{1,0:T(8,128)(4,1)S(1)} %copy-done.18), kind=kLoop, calls=%fused_computation.3 | loop fusion | flops 37748736 | bytes 63488000 | tf_op jit(solution)/shard_map/convert_element_type | solution.py:207
  625.4 13.9 %fusion.94 = bf16[12,64,1024]{2,1,0:T(8,128)(2,1)} fusion(bf16[512,12,64]{0,2,1:T(8,128)(2,1)S(1)} %bitcast.308, f32[12,512]{1,0:T(8,128)S(1)} %log_add_fusion.1, f32[12,512,1024]{2,1,0:T(8,128)} %get-tuple-element.93, pred[512,1024]{1,0:T(8,128)(4,1)S(1)} %copy-done.18), kind=kOutput, calls=%fused_computation.129 | convolution fusion | flops 831258624 | bytes 28073984 | tf_op jit(solution)/shard_map/hqk,qhd->khd/dot_general | solution.py:216
  640.8 17.9 %multiply_reduce_fusion = (f32[12,512]{1,0:T(8,128)S(1)}, f32[12,512,1024]{2,1,0:T(8,128)}) fusion(f32[12,512]{1,0:T(8,128)S(1)} %log_add_fusion, f32[12,512,1024]{2,1,0:T(8,128)} %get-tuple-element.97, pred[512,1024]{1,0:T(8,128)(4,1)S(1)} %copy-done.16, bf16[512,12,64]{0,2,1:T(8,128)(2,1)} %bitcast.305, bf16[1024,12,64]{0,2,1:T(8,128)(2,1)S(1)} %bitcast.300), kind=kOutput, calls=%fused_computation.1 | convolution fusion | flops 836757504 | bytes 53264384 | tf_op jit(solution)/shard_map/qhd,khd->hqk/dot_general | solution.py:203
  658.6 16.9 %multiply_convert_fusion = bf16[12,512,1024]{2,1,0:T(8,128)(2,1)S(1)} fusion(f32[12,512,1024]{2,1,0:T(8,128)} %get-tuple-element.105, f32[12,512]{1,0:T(8,128)S(1)} %get-tuple-element.104, f32[12,512]{1,0:T(8,128)S(1)} %log_add_fusion, f32[12,512,1024]{2,1,0:T(8,128)} %get-tuple-element.97, pred[512,1024]{1,0:T(8,128)(4,1)S(1)} %copy-done.16), kind=kLoop, calls=%fused_computation | loop fusion | flops 37748736 | bytes 63488000 | tf_op jit(solution)/shard_map/convert_element_type | solution.py:207
  680.6 13.1 %fusion.97 = bf16[12,64,1024]{2,1,0:T(8,128)(2,1)} fusion(bf16[512,12,64]{0,2,1:T(8,128)(2,1)S(1)} %bitcast.306, f32[12,512]{1,0:T(8,128)S(1)} %log_add_fusion, f32[12,512,1024]{2,1,0:T(8,128)} %get-tuple-element.97, pred[512,1024]{1,0:T(8,128)(4,1)S(1)} %copy-done.16), kind=kOutput, calls=%fused_computation.130 | convolution fusion | flops 831258624 | bytes 28073984 | tf_op jit(solution)/shard_map/hqk,qhd->khd/dot_general | solution.py:216
  693.8 8.8 fusion.182
  702.6 10.9 %add_convert_fusion = bf16[768,3072]{1,0:T(8,128)(2,1)} fusion(f32[768,3072]{1,0:T(8,128)S(1)} %fusion.182, bf16[1024,768]{1,0:T(8,128)(2,1)} %bitcast.53, f32[1024,3072]{1,0:T(8,128)} %copy-done.93), kind=kOutput, calls=%fused_computation.42 | convolution fusion | flops 4864868352 | bytes 28311552 | tf_op jit(solution)/shard_map/dot_general | solution.py:36
  721.4 10.0 %add_convert_fusion.1 = bf16[768,3072]{1,0:T(8,128)(2,1)} fusion(f32[768,3072]{1,0:T(8,128)S(1)} %fusion.193, bf16[1024,768]{1,0:T(8,128)(2,1)} %bitcast.30, bf16[1024,3072]{1,0:T(8,128)(2,1)} %copy-done.27), kind=kOutput, calls=%fused_computation.43 | convolution fusion | flops 4836556800 | bytes 22020096 | tf_op jit(solution)/shard_map/dot_general | solution.py:36
  737.2 10.2 %multiply_convert_fusion.7 = bf16[12,64,512]{2,1,0:T(8,128)(2,1)} fusion(bf16[1024,12,64]{0,2,1:T(8,128)(2,1)S(1)} %bitcast.292, bf16[12,512,1024]{2,1,0:T(8,128)(2,1)} %copy-done.2), kind=kOutput, calls=%fused_computation.151 | convolution fusion | flops 806092800 | bytes 14942208 | tf_op jit(solution)/shard_map/hqk,khd->qhd/dot_general | solution.py:209
  747.4 9.5 multiply_convert_fusion.6
  763.9 8.8 convolution_add_fusion
  786.4 45.6 %all-reduce.3 = (f32[768]{0:T(1024)S(1)}, f32[768]{0:T(1024)S(1)}, f32[768,16]{0,1:T(8,128)S(1)}) all-reduce(f32[768]{0:T(1024)S(1)} %add.227, f32[768]{0:T(1024)S(1)} %add.230, f32[768,16]{0,1:T(8,128)S(1)} %convolution_add_fusion.2), channel_id=10, replica_groups=mesh['ctx'=2,'shard'=16] {'ctx','shard'}, use_global_device_ids=true, to_apply=%region_38.39.clone | all-reduce | flops 13824 | bytes 110592
  854.4 123.8 %reduce-scatter.18.cloned.1.call-done = f32[24,2304]{1,0:T(8,128)} async-done(((f32[768,2304]{1,0:T(8,128)}), f32[24,2304]{1,0:T(8,128)}) %reduce-scatter.18.cloned.1.call-update) | async-done | bytes 221200 | tf_op jit(solution)/shard_map/reduce_scatter | solution.py:246
  (346 shorter events, 286.2 us)
Async XLA Ops:
  7.2 355.7 %copy-start = (bf16[768,16]{0,1:T(8,128)(2,1)S(1)}, bf16[768,16]{0,1:T(8,128)(2,1)}, u32[]{:S(2)}) copy-start(bf16[768,16]{0,1:T(8,128)(2,1)} %param.21) | copy-start | bytes 73732
  7.2 77.6 %all-gather.11.cloned.1.call-start = ((), (), s32[]{:S(2)}) async-start(), calls=%async_computation.16 | async-start | bytes 3760128 | tf_op jit(solution)/shard_map/all_gather | solution.py:66
  7.9 103.4 %all-gather.21.cloned.1.call-start = ((), (), s32[]{:S(2)}) async-start(), calls=%async_computation.21 | async-start | bytes 2359296 | tf_op jit(solution)/shard_map/all_gather | solution.py:100
  8.7 84.2 %copy-start.50 = (f32[768]{0:T(1024)}, f32[768]{0:T(1024)S(1)}, u32[]{:S(2)}) copy-start(f32[768]{0:T(1024)S(1)} %convert_element_type.215) | copy-start | bytes 9220
  10.3 82.5 %copy-start.63 = (f32[512]{0:T(512)}, f32[512]{0:T(512)S(1)}, u32[]{:S(2)}) copy-start(f32[512]{0:T(512)S(1)} %get-tuple-element.108) | copy-start | bytes 6148
  11.0 81.9 %copy-start.65 = (f32[512]{0:T(512)}, f32[512]{0:T(512)S(1)}, u32[]{:S(2)}) copy-start(f32[512]{0:T(512)S(1)} %get-tuple-element.50) | copy-start | bytes 6148
  90.3 47.4 %all-gather.19.cloned.1.call-start = ((), (), s32[]{:S(2)}) async-start(), calls=%async_computation.20 | async-start | bytes 2359296 | tf_op jit(solution)/shard_map/all_gather | solution.py:101
  91.0 80.9 %all-gather.17.cloned.1.call-start = ((), (), s32[]{:S(2)}) async-start(), calls=%async_computation.19 | async-start | bytes 1253376 | tf_op jit(solution)/shard_map/all_gather | solution.py:67
  91.6 91.0 %all-gather.15.cloned.1.call-start = ((), (), s32[]{:S(2)}) async-start(), calls=%async_computation.18 | async-start | bytes 2359296 | tf_op jit(solution)/shard_map/all_gather | solution.py:100
  91.7 443.0 %copy-start.57 = (s32[1,1,512,1]{2,3,1,0:T(1,128)}, s32[1,1,512,1]{2,3,1,0:T(1,128)S(1)}, u32[]{:S(2)}) copy-start(s32[1,1,512,1]{2,3,1,0:T(1,128)S(1)} %get-tuple-element.78) | copy-start | bytes 6148
  98.4 113.7 %all-gather.13.cloned.1.call-start = ((), (), s32[]{:S(2)}) async-start(), calls=%async_computation.17 | async-start | bytes 2359296 | tf_op jit(solution)/shard_map/all_gather | solution.py:101
  228.8 134.1 %copy-start.21 = (bf16[512,768]{1,0:T(8,128)(2,1)}, bf16[512,768]{1,0:T(8,128)(2,1)S(1)}, u32[]{:S(2)}) copy-start(bf16[512,768]{1,0:T(8,128)(2,1)S(1)} %get-tuple-element.81) | copy-start | bytes 2359300
  228.8 182.1 %copy-start.23 = (bf16[512,768]{1,0:T(8,128)(2,1)}, bf16[512,768]{1,0:T(8,128)(2,1)S(1)}, u32[]{:S(2)}) copy-start(bf16[512,768]{1,0:T(8,128)(2,1)S(1)} %get-tuple-element.80) | copy-start | bytes 2359300
  230.9 41.2 %all-to-all-start.2 = ((bf16[16,64,768]{2,1,0:T(8,128)(2,1)}), bf16[16,64,768]{2,1,0:T(8,128)(2,1)}, u32[]{:S(2)}, u32[]{:S(2)}) async-start(bf16[16,64,768]{2,1,0:T(8,128)(2,1)} %bitcast.313), calls=%async_computation.2 | async-start | bytes 3145728 | tf_op jit(solution)/shard_map/all_to_all | solution.py:141
  272.1 42.1 %all-to-all-start = ((bf16[16,64,768]{2,1,0:T(8,128)(2,1)}), bf16[16,64,768]{2,1,0:T(8,128)(2,1)}, u32[]{:S(2)}, u32[]{:S(2)}) async-start(bf16[16,64,768]{2,1,0:T(8,128)(2,1)} %bitcast.316), calls=%async_computation | async-start | bytes 3145728 | tf_op jit(solution)/shard_map/all_to_all | solution.py:141
  314.3 41.0 %all-to-all-start.3 = ((bf16[16,64,768]{2,1,0:T(8,128)(2,1)}), bf16[16,64,768]{2,1,0:T(8,128)(2,1)}, u32[]{:S(2)}, u32[]{:S(2)}) async-start(bf16[16,64,768]{2,1,0:T(8,128)(2,1)} %bitcast.317), calls=%async_computation.3 | async-start | bytes 3145728 | tf_op jit(solution)/shard_map/all_to_all | solution.py:148
  355.3 41.1 %all-to-all-start.1 = ((bf16[16,64,768]{2,1,0:T(8,128)(2,1)}), bf16[16,64,768]{2,1,0:T(8,128)(2,1)}, u32[]{:S(2)}, u32[]{:S(2)}) async-start(bf16[16,64,768]{2,1,0:T(8,128)(2,1)} %bitcast.315), calls=%async_computation.1 | async-start | bytes 3145728 | tf_op jit(solution)/shard_map/all_to_all | solution.py:148
  401.2 135.1 %copy-start.77 = (f32[512]{0:T(512)}, f32[512]{0:T(512)S(1)}, u32[]{:S(2)}) copy-start(f32[512]{0:T(512)S(1)} %get-tuple-element.88) | copy-start | bytes 6148
  403.5 40.9 %all-to-all-start.6 = ((bf16[16,64,768]{2,1,0:T(8,128)(2,1)}), bf16[16,64,768]{2,1,0:T(8,128)(2,1)}, u32[]{:S(2)}, u32[]{:S(2)}) async-start(bf16[16,64,768]{2,1,0:T(8,128)(2,1)} %bitcast.318), calls=%async_computation.8 | async-start | bytes 3145728 | tf_op jit(solution)/shard_map/all_to_all | solution.py:165
  411.3 156.5 %copy-start.79 = (f32[512]{0:T(512)}, f32[512]{0:T(512)S(1)}, u32[]{:S(2)}) copy-start(f32[512]{0:T(512)S(1)} %get-tuple-element.86) | copy-start | bytes 6148
  444.5 41.2 %all-to-all-start.4 = ((bf16[16,64,768]{2,1,0:T(8,128)(2,1)}), bf16[16,64,768]{2,1,0:T(8,128)(2,1)S(1)}, u32[]{:S(2)}, u32[]{:S(2)}) async-start(bf16[16,64,768]{2,1,0:T(8,128)(2,1)} %bitcast.319), calls=%async_computation.4 | async-start | bytes 3145728 | tf_op jit(solution)/shard_map/all_to_all | solution.py:165
  485.7 41.1 %all-to-all-start.7 = ((bf16[16,64,768]{2,1,0:T(8,128)(2,1)}), bf16[16,64,768]{2,1,0:T(8,128)(2,1)}, u32[]{:S(2)}, u32[]{:S(2)}) async-start(bf16[16,64,768]{2,1,0:T(8,128)(2,1)} %bitcast.320), calls=%async_computation.9 | async-start | bytes 3145728 | tf_op jit(solution)/shard_map/all_to_all | solution.py:181
  526.8 40.9 %all-to-all-start.5 = ((bf16[16,64,768]{2,1,0:T(8,128)(2,1)}), bf16[16,64,768]{2,1,0:T(8,128)(2,1)}, u32[]{:S(2)}, u32[]{:S(2)}) async-start(bf16[16,64,768]{2,1,0:T(8,128)(2,1)} %bitcast.314), calls=%async_computation.5 | async-start | bytes 3145728 | tf_op jit(solution)/shard_map/all_to_all | solution.py:181
  534.2 222.7 %reduce-scatter.10.cloned.1.call-start = ((), (), s32[]{:S(2)}) async-start(), calls=%async_computation.22 | async-start | bytes 2359296 | tf_op jit(solution)/shard_map/reduce_scatter | solution.py:223
  622.0 135.0 %reduce-scatter.12.cloned.1.call-start = ((), (), s32[]{:S(2)}) async-start(), calls=%async_computation.23 | async-start | bytes 2359296 | tf_op jit(solution)/shard_map/reduce_scatter | solution.py:229
  639.4 124.5 %reduce-scatter.14.cloned.1.call-start = ((), (), s32[]{:S(2)}) async-start(), calls=%async_computation.24 | async-start | bytes 2359296 | tf_op jit(solution)/shard_map/reduce_scatter | solution.py:223
  680.5 83.3 %reduce-scatter.16.cloned.1.call-start = ((), (), s32[]{:S(2)}) async-start(), calls=%async_computation.25 | async-start | bytes 2359296 | tf_op jit(solution)/shard_map/reduce_scatter | solution.py:229
  693.7 145.6 %reduce-scatter.24.cloned.1.call-start = ((), (), s32[]{:S(2)}) async-start(), calls=%async_computation.29 | async-start | bytes 7077888 | tf_op jit(solution)/shard_map/reduce_scatter | solution.py:255
  713.6 136.3 %reduce-scatter.22.cloned.1.call-start = ((), (), s32[]{:S(2)}) async-start(), calls=%async_computation.28 | async-start | bytes 7077888 | tf_op jit(solution)/shard_map/reduce_scatter | solution.py:252
  731.4 123.0 %reduce-scatter.20.cloned.1.call-start = ((), (), s32[]{:S(2)}) async-start(), calls=%async_computation.27 | async-start | bytes 2433024 | tf_op jit(solution)/shard_map/reduce_scatter | solution.py:247
  735.8 242.4 %reduce-scatter.18.cloned.1.call-start = ((), (), s32[]{:S(2)}) async-start(), calls=%async_computation.26 | async-start | bytes 7299072 | tf_op jit(solution)/shard_map/reduce_scatter | solution.py:246
  843.8 134.3 %copy-start.1 = (bf16[768,16]{0,1:T(8,128)(2,1)S(1)}, bf16[768,16]{0,1:T(8,128)(2,1)}, u32[]{:S(2)}) copy-start(bf16[768,16]{0,1:T(8,128)(2,1)} %param.21) | copy-start | bytes 73732
  (85 other events, 837.3 us)
Sparse Core Ops, SparseCore 0:
  10.8 73.9 all-gather.10
  90.4 8.3 all-gather.20
  100.9 10.9 all-gather.18
  114.6 57.2 all-gather.16
  173.9 8.6 all-gather.14
  184.6 10.9 all-gather.12
  622.1 10.7 reduce-scatter.9
  639.5 10.7 reduce-scatter.11
  680.7 11.1 reduce-scatter.13
  694.6 11.0 reduce-scatter.15
  713.7 15.1 reduce-scatter.23
  731.7 14.8 reduce-scatter.21
  752.5 100.3 reduce-scatter.19
  859.9 118.1 reduce-scatter.17
where the time goes:
time: 992 us; the launch traced here: 985 us
  waiting for transfers between devices  381 us (38%)
  matrix products  336 us (34%)
  other arithmetic  88.3 us (9%)
  starting transfers between devices  60.9 us (6%)
  blocking collectives  53.2 us (5%)
  local copies, waits for them, and re-layouts  49.9 us (5%)
  between operations  15.8 us (2%)
    reduce_scatter x1, waiting for transfers between devices, body(): lax.psum_scatter(grad_qkv_sum, ('ctx', 'shard'), scatter_dimension=0, til...  124 us
    dot_general x12, matrix products, rows_first(): lax.dot_general(left, right, (((0,), (0,)), ((), ())), preferred_element_...  73.9 us
    all_gather x1, waiting for transfers between devices, body(): lax.all_gather(qkv_weight, 'shard', axis=0, tiled=True)  73.8 us
    dot_general x8, matrix products, rows_last(): lax.dot_general(left, right, (((1,), (1,)), ((), ())), preferred_element_...  57.5 us
    unnamed x1, blocking collectives  45.6 us
    all_to_all x2, waiting for transfers between devices, body(): lax.all_to_all(outbound, 'shard', split_axis=0, concat_axis=0, tiled=True)  41.8 us
    all_to_all x2, waiting for transfers between devices, body(): lax.all_to_all(result.reshape(received.shape), 'shard', split_axis=0, con...  40.4 us
    all_to_all x2, waiting for transfers between devices, body(): lax.all_to_all(grad_outbound.reshape(experts, capacity, D), 'shard', spli...  36.7 us
  transfers between devices with their start and end apart: 22, of which 12 were waited for; matrix products, arithmetic and copies ran while one was open for 37% of the time, Pallas kernels for 0%

commit v1 on v0

--- a/solution.py
+++ b/solution.py
@@ -11,6 +11,17 @@
 EPSILON = 1e-05
 NEGATIVE = -1e30
 HIGH = lax.Precision.HIGHEST
+
+
+def split_up(shard, dim, size):
+    before, after = (shard.shape[:dim], shard.shape[dim + 1 :])
+    return jnp.moveaxis(shard.reshape(*before, size, -1, *after), dim, 0)
+
+
+def laid_out(parts, dim):
+    shape = list(parts.shape[1:])
+    shape[dim] *= parts.shape[0]
+    return jnp.moveaxis(parts, 0, dim).reshape(shape)
 
 
 def layer_norm(values, gain_vec):
@@ -145,9 +156,15 @@
         result = jnp.dot(hidden, down_local, preferred_element_type=jnp.float32).astype(
             jnp.bfloat16
         )
-        returned = lax.all_to_all(
-            result.reshape(received.shape), "shard", split_axis=0, concat_axis=0, tiled=True
-        )
+        array = result.reshape(received.shape)
+        size, mine = (lax.axis_size("shard"), lax.axis_index("shard"))
+        blocks = split_up(array, 0, size)
+        outs = [blocks[mine]]
+        for step in range(1, size):
+            sent = blocks[mine ^ step]
+            outs.append(lax.ppermute(sent, "shard", [(i, i ^ step) for i in range(size)]))
+        blocks = jnp.stack(outs)[mine ^ jnp.arange(size)]
+        returned = laid_out(blocks, 0)
         returned, received, upward = (
             returned,
             received,

time: 992 us -> 1030 us (1.038)
  starting transfers between devices: 60.9 us -> 105 us
  waiting for transfers between devices: 381 us -> 341 us
  local copies, waits for them, and re-layouts: 49.9 us -> 77.3 us
    ppermute x0 -> x30, starting transfers between devices: none -> 57.1 us  [body(): lax.ppermute(sent, 'shard', [(i, i ^ step) for i in range(size)])]
    all_to_all x2 -> x0, waiting for transfers between devices: 40.4 us -> none  [body(): lax.all_to_all(result.reshape(received.shape), 'shard', split_axis=0, con...]
    unnamed x194 -> x244, local copies, waits for them, and re-layouts: 31.4 us -> 48.8 us
    all_to_all x2 -> x0, starting transfers between devices: 14.9 us -> none  [body(): lax.all_to_all(result.reshape(received.shape), 'shard', split_axis=0, con...]
  transfers between devices with their start and end apart: 22 -> 50, of which waited for: 12 -> 13; matrix products, arithmetic and copies ran while one was open for 37% -> 39% of each run, Pallas kernels for 0% -> 0%
where the time goes in v1:
time: 1030 us; the launch traced here: 1020 us
  waiting for transfers between devices  341 us (33%)
  matrix products  340 us (33%)
  starting transfers between devices  105 us (10%)
  other arithmetic  87 us (8%)
  local copies, waits for them, and re-layouts  77.3 us (8%)
  blocking collectives  51.8 us (5%)
  between operations  16 us (2%)
    reduce_scatter x1, waiting for transfers between devices, body(): lax.psum_scatter(grad_qkv_sum, ('ctx', 'shard'), scatter_dimension=0, til...  123 us
    all_gather x1, waiting for transfers between devices, body(): lax.all_gather(qkv_weight, 'shard', axis=0, tiled=True)  73.8 us
    dot_general x12, matrix products, rows_first(): lax.dot_general(left, right, (((0,), (0,)), ((), ())), preferred_element_...  70.7 us
    dot_general x8, matrix products, rows_last(): lax.dot_general(left, right, (((1,), (1,)), ((), ())), preferred_element_...  57.5 us
    ppermute x30, starting transfers between devices, body(): lax.ppermute(sent, 'shard', [(i, i ^ step) for i in range(size)])  57.1 us
    unnamed x244, local copies, waits for them, and re-layouts  48.8 us
    unnamed x1, blocking collectives  44.5 us
    all_to_all x2, waiting for transfers between devices, body(): lax.all_to_all(grad_send, 'shard', split_axis=0, concat_axis=0, tiled=True)  35.8 us
  transfers between devices with their start and end apart: 50, of which 13 were waited for; matrix products, arithmetic and copies ran while one was open for 39% of the time, Pallas kernels for 0%

profile of v1, /device:TPU:0, one launch (start us, length us, event | category | flops | bytes accessed | tf_op | source)
XLA Modules:
  0.0 1018.4 jit_solution(12546534493265613377)
XLA Ops:
  11.0 73.8 %all-gather.11.cloned.1.call-done = bf16[768,2304]{1,0:T(8,128)(2,1)} async-done(((bf16[48,2304]{1,0:T(8,128)(2,1)}), bf16[768,2304]{1,0:T(8,128)(2,1)}) %all-gather.11.cloned.1.call-update) | async-done | bytes 3538960 | tf_op jit(solution)/shard_map/all_gather | solution.py:77
  112.8 12.8 %fusion.27 = (f32[12,512]{1,0:T(8,128)S(1)}, f32[12,512,1024]{2,1,0:T(8,128)}) fusion(pred[512,1024]{1,0:T(8,128)(4,1)} %get-tuple-element.123, bf16[512,12,64]{0,2,1:T(8,128)(2,1)} %bitcast.417, bf16[1024,12,64]{0,2,1:T(8,128)(2,1)S(1)} %bitcast.413), kind=kOutput, calls=%fused_computation.47 | convolution fusion | flops 824174592 | bytes 28073984 | tf_op jit(solution)/shard_map/qhd,khd->hqk/dot_general | solution.py:38
  125.6 11.8 %fusion.1 = f32[12,512]{1,0:T(8,128)S(1)} fusion(f32[12,512]{1,0:T(8,128)S(1)} %get-tuple-element.128, f32[12,512,1024]{2,1,0:T(8,128)} %get-tuple-element.129, pred[512,1024]{1,0:T(8,128)(4,1)S(1)} %copy-done.14), kind=kLoop, calls=%fused_computation.15 | loop fusion | flops 25159680 | bytes 25739264 | tf_op jit(solution)/shard_map/reduce_sum | solution.py:124
  140.1 12.7 %fusion.112 = bf16[12,64,512]{2,1,0:T(8,128)(2,1)} fusion(bf16[1024,12,64]{0,2,1:T(8,128)(2,1)} %bitcast.423, f32[12,512]{1,0:T(8,128)S(1)} %fusion.1, f32[12,512]{1,0:T(8,128)S(1)} %get-tuple-element.128, f32[12,512,1024]{2,1,0:T(8,128)} %get-tuple-element.129, pred[512,1024]{1,0:T(8,128)(4,1)S(1)} %copy-done.15), kind=kOutput, calls=%fused_computation.164 | convolution fusion | flops 837156864 | bytes 28098560 | tf_op jit(solution)/shard_map/hqk,khd->qhd/dot_general | solution.py:127
  152.8 19.1 %all-gather.17.cloned.1.call-done = bf16[768,768]{1,0:T(8,128)(2,1)} async-done(((bf16[48,768]{1,0:T(8,128)(2,1)}), bf16[768,768]{1,0:T(8,128)(2,1)}) %all-gather.17.cloned.1.call-update) | async-done | bytes 1179664 | tf_op jit(solution)/shard_map/all_gather | solution.py:78
  185.6 15.0 %fusion.26 = (f32[12,512]{1,0:T(8,128)S(1)}, f32[12,512,1024]{2,1,0:T(8,128)}) fusion(pred[512,1024]{1,0:T(8,128)(4,1)} %get-tuple-element.122, bf16[512,12,64]{0,2,1:T(8,128)(2,1)} %bitcast.419, bf16[1024,12,64]{0,2,1:T(8,128)(2,1)} %bitcast.415), kind=kOutput, calls=%fused_computation.46 | convolution fusion | flops 824174592 | bytes 28073984 | tf_op jit(solution)/shard_map/qhd,khd->hqk/dot_general | solution.py:38
  200.5 11.8 %fusion = f32[12,512]{1,0:T(8,128)S(1)} fusion(f32[12,512]{1,0:T(8,128)S(1)} %get-tuple-element.124, f32[12,512,1024]{2,1,0:T(8,128)} %get-tuple-element.125, pred[512,1024]{1,0:T(8,128)(4,1)S(1)} %copy-done.17), kind=kLoop, calls=%fused_computation.14 | loop fusion | flops 25159680 | bytes 25739264 | tf_op jit(solution)/shard_map/reduce_sum | solution.py:124
  214.9 11.9 %fusion.113 = bf16[12,64,512]{2,1,0:T(8,128)(2,1)S(1)} fusion(bf16[1024,12,64]{0,2,1:T(8,128)(2,1)} %bitcast.425, f32[12,512]{1,0:T(8,128)S(1)} %fusion, f32[12,512]{1,0:T(8,128)S(1)} %get-tuple-element.124, f32[12,512,1024]{2,1,0:T(8,128)} %get-tuple-element.125, pred[512,1024]{1,0:T(8,128)(4,1)} %get-tuple-element.122), kind=kOutput, calls=%fused_computation.165 | convolution fusion | flops 837156864 | bytes 28098560 | tf_op jit(solution)/shard_map/hqk,khd->qhd/dot_general | solution.py:127
  242.5 30.0 %all-to-all-done = bf16[16,64,768]{2,1,0:T(8,128)(2,1)} async-done(((bf16[16,64,768]{2,1,0:T(8,128)(2,1)}), bf16[16,64,768]{2,1,0:T(8,128)(2,1)}, u32[]{:S(2)}, u32[]{:S(2)}) %all-to-all-start) | async-done | bytes 1572896 | tf_op jit(solution)/shard_map/all_to_all | solution.py:152
  288.1 13.4 %fusion.88 = bf16[1024,768]{1,0:T(8,128)(2,1)S(1)} fusion(bf16[1,3072,768]{2,1,0:T(8,128)(2,1)} %param.23, f32[1024,3072]{1,0:T(8,128)S(1)} %fusion.42), kind=kOutput, calls=%fused_computation.129 | convolution fusion | flops 4860936192 | bytes 18874368 | tf_op jit(solution)/shard_map/dot_general | solution.py:156
  321.9 13.6 %fusion.91 = bf16[1024,768]{1,0:T(8,128)(2,1)S(1)} fusion(bf16[1,3072,768]{2,1,0:T(8,128)(2,1)} %param.23, f32[1024,3072]{1,0:T(8,128)S(1)} %fusion.40), kind=kOutput, calls=%fused_computation.130 | convolution fusion | flops 4860936192 | bytes 18874368 | tf_op jit(solution)/shard_map/dot_general | solution.py:156
  433.8 9.4 all-to-all-start.4
  447.0 28.0 %all-to-all-done.4 = bf16[16,64,768]{2,1,0:T(8,128)(2,1)} async-done(((bf16[16,64,768]{2,1,0:T(8,128)(2,1)}), bf16[16,64,768]{2,1,0:T(8,128)(2,1)}, u32[]{:S(2)}, u32[]{:S(2)}) %all-to-all-start.4) | async-done | bytes 1572896 | tf_op jit(solution)/shard_map/all_to_all | solution.py:182
  482.8 15.4 %fusion.17 = bf16[1024,3072]{1,0:T(8,128)(2,1)S(1)} fusion(f32[1024,3072]{1,0:T(8,128)} %copy-done.105, bf16[1024,768]{1,0:T(8,128)(2,1)} %bitcast.116, bf16[1,3072,768]{2,1,0:T(8,128)(2,1)} %param.23), kind=kOutput, calls=%fused_computation.35 | convolution fusion | flops 4894752768 | bytes 25165824 | tf_op jit(solution)/shard_map/dot_general | solution.py:53
  500.8 8.5 fusion.85
  524.0 14.2 %fusion.10 = bf16[1024,3072]{1,0:T(8,128)(2,1)S(1)} fusion(f32[1024,3072]{1,0:T(8,128)} %copy-done.104, bf16[1024,768]{1,0:T(8,128)(2,1)S(1)} %bitcast.433, bf16[1,3072,768]{2,1,0:T(8,128)(2,1)} %param.23), kind=kOutput, calls=%fused_computation.28 | convolution fusion | flops 4894752768 | bytes 25165824 | tf_op jit(solution)/shard_map/dot_general | solution.py:53
  540.8 8.5 fusion.82
  571.0 27.5 %all-to-all-done.3 = bf16[16,64,768]{2,1,0:T(8,128)(2,1)} async-done(((bf16[16,64,768]{2,1,0:T(8,128)(2,1)}), bf16[16,64,768]{2,1,0:T(8,128)(2,1)}, u32[]{:S(2)}, u32[]{:S(2)}) %all-to-all-start.3) | async-done | bytes 1572896 | tf_op jit(solution)/shard_map/all_to_all | solution.py:198
  613.1 17.9 %multiply_reduce_fusion.1 = (f32[12,512]{1,0:T(8,128)S(1)}, f32[12,512,1024]{2,1,0:T(8,128)}) fusion(f32[12,512]{1,0:T(8,128)S(1)} %log_add_fusion.1, f32[12,512,1024]{2,1,0:T(8,128)} %get-tuple-element.125, pred[512,1024]{1,0:T(8,128)(4,1)S(1)} %copy-done.18, bf16[512,12,64]{0,2,1:T(8,128)(2,1)} %bitcast.431, bf16[1024,12,64]{0,2,1:T(8,128)(2,1)S(1)} %bitcast.426), kind=kOutput, calls=%fused_computation.6 | convolution fusion | flops 836757504 | bytes 53264384 | tf_op jit(solution)/shard_map/qhd,khd->hqk/dot_general | solution.py:220
  631.0 16.9 %multiply_convert_fusion.1 = bf16[12,512,1024]{2,1,0:T(8,128)(2,1)S(1)} fusion(f32[12,512,1024]{2,1,0:T(8,128)} %get-tuple-element.135, f32[12,512]{1,0:T(8,128)S(1)} %get-tuple-element.134, f32[12,512]{1,0:T(8,128)S(1)} %log_add_fusion.1, f32[12,512,1024]{2,1,0:T(8,128)} %get-tuple-element.125, pred[512,1024]{1,0:T(8,128)(4,1)S(1)} %copy-done.18), kind=kLoop, calls=%fused_computation.5 | loop fusion | flops 37748736 | bytes 63488000 | tf_op jit(solution)/shard_map/convert_element_type | solution.py:224
  657.0 14.3 %fusion.94 = bf16[12,64,1024]{2,1,0:T(8,128)(2,1)} fusion(bf16[512,12,64]{0,2,1:T(8,128)(2,1)} %bitcast.432, f32[12,512]{1,0:T(8,128)S(1)} %log_add_fusion.1, f32[12,512,1024]{2,1,0:T(8,128)} %get-tuple-element.125, pred[512,1024]{1,0:T(8,128)(4,1)S(1)} %copy-done.18), kind=kOutput, calls=%fused_computation.131 | convolution fusion | flops 831258624 | bytes 28073984 | tf_op jit(solution)/shard_map/hqk,qhd->khd/dot_general | solution.py:233
  672.3 17.8 %multiply_reduce_fusion = (f32[12,512]{1,0:T(8,128)S(1)}, f32[12,512,1024]{2,1,0:T(8,128)}) fusion(f32[12,512]{1,0:T(8,128)S(1)} %log_add_fusion, f32[12,512,1024]{2,1,0:T(8,128)} %get-tuple-element.129, pred[512,1024]{1,0:T(8,128)(4,1)S(1)} %copy-done.16, bf16[512,12,64]{0,2,1:T(8,128)(2,1)} %bitcast.429, bf16[1024,12,64]{0,2,1:T(8,128)(2,1)S(1)} %bitcast.424), kind=kOutput, calls=%fused_computation.3 | convolution fusion | flops 836757504 | bytes 53264384 | tf_op jit(solution)/shard_map/qhd,khd->hqk/dot_general | solution.py:220
  690.1 16.9 %multiply_convert_fusion = bf16[12,512,1024]{2,1,0:T(8,128)(2,1)S(1)} fusion(f32[12,512,1024]{2,1,0:T(8,128)} %get-tuple-element.137, f32[12,512]{1,0:T(8,128)S(1)} %get-tuple-element.136, f32[12,512]{1,0:T(8,128)S(1)} %log_add_fusion, f32[12,512,1024]{2,1,0:T(8,128)} %get-tuple-element.129, pred[512,1024]{1,0:T(8,128)(4,1)S(1)} %copy-done.16), kind=kLoop, calls=%fused_computation.2 | loop fusion | flops 37748736 | bytes 63488000 | tf_op jit(solution)/shard_map/convert_element_type | solution.py:224
  713.1 13.4 %fusion.97 = bf16[12,64,1024]{2,1,0:T(8,128)(2,1)} fusion(bf16[512,12,64]{0,2,1:T(8,128)(2,1)S(1)} %bitcast.430, f32[12,512]{1,0:T(8,128)S(1)} %log_add_fusion, f32[12,512,1024]{2,1,0:T(8,128)} %get-tuple-element.129, pred[512,1024]{1,0:T(8,128)(4,1)S(1)} %copy-done.16), kind=kOutput, calls=%fused_computation.132 | convolution fusion | flops 831258624 | bytes 28073984 | tf_op jit(solution)/shard_map/hqk,qhd->khd/dot_general | solution.py:233
  728.0 8.5 fusion.183
  736.4 10.8 %add_convert_fusion = bf16[768,3072]{1,0:T(8,128)(2,1)} fusion(f32[768,3072]{1,0:T(8,128)S(1)} %fusion.183, bf16[1024,768]{1,0:T(8,128)(2,1)} %bitcast.116, f32[1024,3072]{1,0:T(8,128)} %copy-done.105), kind=kOutput, calls=%fused_computation.44 | convolution fusion | flops 4864868352 | bytes 28311552 | tf_op jit(solution)/shard_map/dot_general | solution.py:47
  755.1 9.5 add_convert_fusion.1
  771.3 11.0 %multiply_convert_fusion.7 = bf16[12,64,512]{2,1,0:T(8,128)(2,1)} fusion(bf16[1024,12,64]{0,2,1:T(8,128)(2,1)S(1)} %bitcast.416, bf16[12,512,1024]{2,1,0:T(8,128)(2,1)} %copy-done.2), kind=kOutput, calls=%fused_computation.153 | convolution fusion | flops 806092800 | bytes 14942208 | tf_op jit(solution)/shard_map/hqk,khd->qhd/dot_general | solution.py:226
  782.3 9.5 multiply_convert_fusion.6
  798.8 8.8 convolution_add_fusion
  821.3 44.5 %all-reduce.3 = (f32[768]{0:T(1024)S(1)}, f32[768]{0:T(1024)S(1)}, f32[768,16]{0,1:T(8,128)S(1)}) all-reduce(f32[768]{0:T(1024)S(1)} %add.319, f32[768]{0:T(1024)S(1)} %add.322, f32[768,16]{0,1:T(8,128)S(1)} %convolution_add_fusion.2), channel_id=10, replica_groups=mesh['ctx'=2,'shard'=16] {'ctx','shard'}, use_global_device_ids=true, to_apply=%region_38.39.clone | all-reduce | flops 13824 | bytes 110592
  888.2 123.3 %reduce-scatter.18.cloned.1.call-done = f32[24,2304]{1,0:T(8,128)} async-done(((f32[768,2304]{1,0:T(8,128)}), f32[24,2304]{1,0:T(8,128)}) %reduce-scatter.18.cloned.1.call-update) | async-done | bytes 221200 | tf_op jit(solution)/shard_map/reduce_scatter | solution.py:263
  (460 shorter events, 342.1 us)
Async XLA Ops:
  7.2 77.6 %all-gather.11.cloned.1.call-start = ((), (), s32[]{:S(2)}) async-start(), calls=%async_computation.14 | async-start | bytes 3760128 | tf_op jit(solution)/shard_map/all_gather | solution.py:77
  7.9 103.2 %all-gather.21.cloned.1.call-start = ((), (), s32[]{:S(2)}) async-start(), calls=%async_computation.19 | async-start | bytes 2359296 | tf_op jit(solution)/shard_map/all_gather | solution.py:111
  90.3 47.2 %all-gather.19.cloned.1.call-start = ((), (), s32[]{:S(2)}) async-start(), calls=%async_computation.18 | async-start | bytes 2359296 | tf_op jit(solution)/shard_map/all_gather | solution.py:112
  91.0 80.9 %all-gather.17.cloned.1.call-start = ((), (), s32[]{:S(2)}) async-start(), calls=%async_computation.17 | async-start | bytes 1253376 | tf_op jit(solution)/shard_map/all_gather | solution.py:78
  91.6 91.0 %all-gather.15.cloned.1.call-start = ((), (), s32[]{:S(2)}) async-start(), calls=%async_computation.16 | async-start | bytes 2359296 | tf_op jit(solution)/shard_map/all_gather | solution.py:111
  98.4 113.9 %all-gather.13.cloned.1.call-start = ((), (), s32[]{:S(2)}) async-start(), calls=%async_computation.15 | async-start | bytes 2359296 | tf_op jit(solution)/shard_map/all_gather | solution.py:112
  231.2 41.3 %all-to-all-start = ((bf16[16,64,768]{2,1,0:T(8,128)(2,1)}), bf16[16,64,768]{2,1,0:T(8,128)(2,1)}, u32[]{:S(2)}, u32[]{:S(2)}) async-start(bf16[16,64,768]{2,1,0:T(8,128)(2,1)} %bitcast.435), calls=%async_computation | async-start | bytes 3145728 | tf_op jit(solution)/shard_map/all_to_all | solution.py:152
  272.5 42.0 %all-to-all-start.1 = ((bf16[16,64,768]{2,1,0:T(8,128)(2,1)}), bf16[16,64,768]{2,1,0:T(8,128)(2,1)}, u32[]{:S(2)}, u32[]{:S(2)}) async-start(bf16[16,64,768]{2,1,0:T(8,128)(2,1)} %bitcast.438), calls=%async_computation.1 | async-start | bytes 3145728 | tf_op jit(solution)/shard_map/all_to_all | solution.py:152
  302.6 33.8 %collective-permute-start = (bf16[1,64,768]{2,1,0:T(8,128)(2,1)}, bf16[1,64,768]{2,1,0:T(8,128)(2,1)}, u32[]{:S(2)}, u32[]{:S(2)}) collective-permute-start(bf16[1,64,768]{2,1,0:T(8,128)(2,1)} %get-tuple-element.87), channel_id=1, source_target_pairs={{0,1},{1,0},{2,3},{3,2},{4,5},{5,4},{6,7},{7,6},{8,9},{9,8},{10,11... | collective-permute-start | bytes 294920 | tf_op jit(solution)/shard_map/ppermute | solution.py:165
  304.5 39.3 %collective-permute-start.1 = (bf16[1,64,768]{2,1,0:T(8,128)(2,1)}, bf16[1,64,768]{2,1,0:T(8,128)(2,1)}, u32[]{:S(2)}, u32[]{:S(2)}) collective-permute-start(bf16[1,64,768]{2,1,0:T(8,128)(2,1)} %get-tuple-element.86), channel_id=1, source_target_pairs={{0,2},{1,3},{2,0},{3,1},{4,6},{5,7},{6,4},{7,5},{8,10},{9,11},{10,... | collective-permute-start | bytes 294920 | tf_op jit(solution)/shard_map/ppermute | solution.py:165
  305.9 39.4 %collective-permute-start.2 = (bf16[1,64,768]{2,1,0:T(8,128)(2,1)}, bf16[1,64,768]{2,1,0:T(8,128)(2,1)}, u32[]{:S(2)}, u32[]{:S(2)}) collective-permute-start(bf16[1,64,768]{2,1,0:T(8,128)(2,1)} %get-tuple-element.85), channel_id=1, source_target_pairs={{0,3},{1,2},{2,1},{3,0},{4,7},{5,6},{6,5},{7,4},{8,11},{9,10},{10,... | collective-permute-start | bytes 294920 | tf_op jit(solution)/shard_map/ppermute | solution.py:165
  306.1 44.1 %collective-permute-start.3 = (bf16[1,64,768]{2,1,0:T(8,128)(2,1)}, bf16[1,64,768]{2,1,0:T(8,128)(2,1)}, u32[]{:S(2)}, u32[]{:S(2)}) collective-permute-start(bf16[1,64,768]{2,1,0:T(8,128)(2,1)} %get-tuple-element.84), channel_id=1, source_target_pairs={{0,4},{1,5},{2,6},{3,7},{4,0},{5,1},{6,2},{7,3},{8,12},{9,13},{10,... | collective-permute-start | bytes 294920 | tf_op jit(solution)/shard_map/ppermute | solution.py:165
  307.9 44.2 %collective-permute-start.4 = (bf16[1,64,768]{2,1,0:T(8,128)(2,1)}, bf16[1,64,768]{2,1,0:T(8,128)(2,1)}, u32[]{:S(2)}, u32[]{:S(2)}) collective-permute-start(bf16[1,64,768]{2,1,0:T(8,128)(2,1)} %get-tuple-element.83), channel_id=1, source_target_pairs={{0,5},{1,4},{2,7},{3,6},{4,1},{5,0},{6,3},{7,2},{8,13},{9,12},{10,... | collective-permute-start | bytes 294920 | tf_op jit(solution)/shard_map/ppermute | solution.py:165
  336.4 18.4 %collective-permute-start.5 = (bf16[1,64,768]{2,1,0:T(8,128)(2,1)S(1)}, bf16[1,64,768]{2,1,0:T(8,128)(2,1)S(1)}, u32[]{:S(2)}, u32[]{:S(2)}) collective-permute-start(bf16[1,64,768]{2,1,0:T(8,128)(2,1)S(1)} %copy-done.69), channel_id=1, source_target_pairs={{0,6},{1,7},{2,4},{3,5},{4,2},{5,3},{6,0},{7,1},{8,14},{9,15},{10,... | collective-permute-start | bytes 294920 | tf_op jit(solution)/shard_map/ppermute | solution.py:165
  352.2 17.4 %collective-permute-start.9 = (bf16[1,64,768]{2,1,0:T(8,128)(2,1)S(1)}, bf16[1,64,768]{2,1,0:T(8,128)(2,1)S(1)}, u32[]{:S(2)}, u32[]{:S(2)}) collective-permute-start(bf16[1,64,768]{2,1,0:T(8,128)(2,1)S(1)} %copy-done.65), channel_id=1, source_target_pairs={{0,10},{1,11},{2,8},{3,9},{4,14},{5,15},{6,12},{7,13},{8,2},{9,3},... | collective-permute-start | bytes 294920 | tf_op jit(solution)/shard_map/ppermute | solution.py:165
  354.8 19.8 %collective-permute-start.10 = (bf16[1,64,768]{2,1,0:T(8,128)(2,1)S(1)}, bf16[1,64,768]{2,1,0:T(8,128)(2,1)S(1)}, u32[]{:S(2)}, u32[]{:S(2)}) collective-permute-start(bf16[1,64,768]{2,1,0:T(8,128)(2,1)S(1)} %copy-done.64), channel_id=1, source_target_pairs={{0,11},{1,10},{2,9},{3,8},{4,15},{5,14},{6,13},{7,12},{8,3},{9,2},... | collective-permute-start | bytes 294920 | tf_op jit(solution)/shard_map/ppermute | solution.py:165
  389.5 17.9 %collective-permute-start.22 = (bf16[1,64,768]{2,1,0:T(8,128)(2,1)S(1)}, bf16[1,64,768]{2,1,0:T(8,128)(2,1)S(1)}, u32[]{:S(2)}, u32[]{:S(2)}) collective-permute-start(bf16[1,64,768]{2,1,0:T(8,128)(2,1)S(1)} %get-tuple-element.96), channel_id=1, source_target_pairs={{0,8},{1,9},{2,10},{3,11},{4,12},{5,13},{6,14},{7,15},{8,0},{9,1},... | collective-permute-start | bytes 294920 | tf_op jit(solution)/shard_map/ppermute | solution.py:165
  391.2 19.2 %collective-permute-start.23 = (bf16[1,64,768]{2,1,0:T(8,128)(2,1)S(1)}, bf16[1,64,768]{2,1,0:T(8,128)(2,1)S(1)}, u32[]{:S(2)}, u32[]{:S(2)}) collective-permute-start(bf16[1,64,768]{2,1,0:T(8,128)(2,1)S(1)} %get-tuple-element.95), channel_id=1, source_target_pairs={{0,9},{1,8},{2,11},{3,10},{4,13},{5,12},{6,15},{7,14},{8,1},{9,0},... | collective-permute-start | bytes 294920 | tf_op jit(solution)/shard_map/ppermute | solution.py:165
  394.3 18.1 %collective-permute-start.24 = (bf16[1,64,768]{2,1,0:T(8,128)(2,1)S(1)}, bf16[1,64,768]{2,1,0:T(8,128)(2,1)S(1)}, u32[]{:S(2)}, u32[]{:S(2)}) collective-permute-start(bf16[1,64,768]{2,1,0:T(8,128)(2,1)S(1)} %get-tuple-element.94), channel_id=1, source_target_pairs={{0,10},{1,11},{2,8},{3,9},{4,14},{5,15},{6,12},{7,13},{8,2},{9,3},... | collective-permute-start | bytes 294920 | tf_op jit(solution)/shard_map/ppermute | solution.py:165
  396.7 19.8 %collective-permute-start.25 = (bf16[1,64,768]{2,1,0:T(8,128)(2,1)S(1)}, bf16[1,64,768]{2,1,0:T(8,128)(2,1)S(1)}, u32[]{:S(2)}, u32[]{:S(2)}) collective-permute-start(bf16[1,64,768]{2,1,0:T(8,128)(2,1)S(1)} %get-tuple-element.93), channel_id=1, source_target_pairs={{0,11},{1,10},{2,9},{3,8},{4,15},{5,14},{6,13},{7,12},{8,3},{9,2},... | collective-permute-start | bytes 294920 | tf_op jit(solution)/shard_map/ppermute | solution.py:165
  433.8 41.3 %all-to-all-start.4 = ((bf16[16,64,768]{2,1,0:T(8,128)(2,1)}), bf16[16,64,768]{2,1,0:T(8,128)(2,1)}, u32[]{:S(2)}, u32[]{:S(2)}) async-start(bf16[16,64,768]{2,1,0:T(8,128)(2,1)} %bitcast.441), calls=%async_computation.6 | async-start | bytes 3145728 | tf_op jit(solution)/shard_map/all_to_all | solution.py:182
  475.1 41.1 %all-to-all-start.2 = ((bf16[16,64,768]{2,1,0:T(8,128)(2,1)}), bf16[16,64,768]{2,1,0:T(8,128)(2,1)S(1)}, u32[]{:S(2)}, u32[]{:S(2)}) async-start(bf16[16,64,768]{2,1,0:T(8,128)(2,1)} %bitcast.442), calls=%async_computation.2 | async-start | bytes 3145728 | tf_op jit(solution)/shard_map/all_to_all | solution.py:182
  516.2 41.4 %all-to-all-start.5 = ((bf16[16,64,768]{2,1,0:T(8,128)(2,1)}), bf16[16,64,768]{2,1,0:T(8,128)(2,1)}, u32[]{:S(2)}, u32[]{:S(2)}) async-start(bf16[16,64,768]{2,1,0:T(8,128)(2,1)} %bitcast.443), calls=%async_computation.7 | async-start | bytes 3145728 | tf_op jit(solution)/shard_map/all_to_all | solution.py:198
  557.6 40.9 %all-to-all-start.3 = ((bf16[16,64,768]{2,1,0:T(8,128)(2,1)}), bf16[16,64,768]{2,1,0:T(8,128)(2,1)}, u32[]{:S(2)}, u32[]{:S(2)}) async-start(bf16[16,64,768]{2,1,0:T(8,128)(2,1)} %bitcast.103), calls=%async_computation.3 | async-start | bytes 3145728 | tf_op jit(solution)/shard_map/all_to_all | solution.py:198
  565.0 226.9 %reduce-scatter.10.cloned.1.call-start = ((), (), s32[]{:S(2)}) async-start(), calls=%async_computation.20 | async-start | bytes 2359296 | tf_op jit(solution)/shard_map/reduce_scatter | solution.py:240
  653.0 138.9 %reduce-scatter.12.cloned.1.call-start = ((), (), s32[]{:S(2)}) async-start(), calls=%async_computation.21 | async-start | bytes 2359296 | tf_op jit(solution)/shard_map/reduce_scatter | solution.py:246
  671.3 127.5 %reduce-scatter.14.cloned.1.call-start = ((), (), s32[]{:S(2)}) async-start(), calls=%async_computation.22 | async-start | bytes 2359296 | tf_op jit(solution)/shard_map/reduce_scatter | solution.py:240
  712.0 86.7 %reduce-scatter.16.cloned.1.call-start = ((), (), s32[]{:S(2)}) async-start(), calls=%async_computation.23 | async-start | bytes 2359296 | tf_op jit(solution)/shard_map/reduce_scatter | solution.py:246
  726.6 146.5 %reduce-scatter.24.cloned.1.call-start = ((), (), s32[]{:S(2)}) async-start(), calls=%async_computation.27 | async-start | bytes 7077888 | tf_op jit(solution)/shard_map/reduce_scatter | solution.py:272
  747.3 136.3 %reduce-scatter.22.cloned.1.call-start = ((), (), s32[]{:S(2)}) async-start(), calls=%async_computation.26 | async-start | bytes 7077888 | tf_op jit(solution)/shard_map/reduce_scatter | solution.py:269
  764.7 123.5 %reduce-scatter.20.cloned.1.call-start = ((), (), s32[]{:S(2)}) async-start(), calls=%async_computation.25 | async-start | bytes 2433024 | tf_op jit(solution)/shard_map/reduce_scatter | solution.py:264
  770.0 241.5 %reduce-scatter.18.cloned.1.call-start = ((), (), s32[]{:S(2)}) async-start(), calls=%async_computation.24 | async-start | bytes 7299072 | tf_op jit(solution)/shard_map/reduce_scatter | solution.py:263
  (124 other events, 2750.0 us)
Sparse Core Ops, SparseCore 0:
  10.8 73.9 all-gather.10
  90.4 8.3 all-gather.20
  100.9 10.9 all-gather.18
  114.6 57.2 all-gather.16
  173.9 8.6 all-gather.14
  184.5 10.9 all-gather.12
  653.1 10.7 reduce-scatter.9
  671.4 10.6 reduce-scatter.11
  712.2 10.9 reduce-scatter.13
  726.7 11.1 reduce-scatter.15
  747.4 14.5 reduce-scatter.23
  764.9 15.0 reduce-scatter.21
  785.8 100.3 reduce-scatter.19
  893.2 118.1 reduce-scatter.17
